TPU v7x, 32 devices: a whole 2x2x4 slice. The times are simulated.
32 devices in a mesh: seq: 8 (over z, x), chan: 4 (over y, core).
Axes of the slice: x: 2, y: 2, z: 4, core: 2. Of those that a mesh axis runs over, the one named last changes fastest.
Arguments:
- signal: float32 [256, 65536], P('chan', 'seq'), may hold values from -6 to 6
- gating: float32 [256, 65536], P('chan', 'seq'), may hold values from -6 to 6
- response: float32 [256, 65536], P('chan', 'seq'), may hold values from -0.0234375 to 0.0234375
- skip_gain: float32 [256], P('chan'), may hold values from -4 to 4
- mixing_weight: float32 [256, 256], P(None, 'chan'), may hold values from -0.5 to 0.5
Outputs:
- output: float32 [256, 65536], P('chan', 'seq')
All inputs are finite; a program needn't handle non-finite values.
Results may differ from a plain program's by a relative error of at most 0.00007.
Values sent between devices are 32-bit elements; how exact they have to be, the bound alone decides.
A program may use at most 128 MiB of HBM per device.

v0:
```python
from functools import partial
import math

import jax
import jax.numpy as jnp
import numpy as np
from jax import lax
from jax.sharding import PartitionSpec as P


def twiddle(number, period):
    angle = (number % period).astype(jnp.float32) * (2.0 * math.pi / period)
    return (jnp.cos(angle), jnp.sin(angle))


def rotate(real_part, imag_part, cos_part, sin_part):
    return (
        real_part * cos_part - imag_part * sin_part,
        imag_part * cos_part + real_part * sin_part,
    )


def dft_table(length, sign):
    steps = jnp.arange(length, dtype=jnp.int32)
    cos_part, sin_part = twiddle(steps[:, None] * steps[None, :], length)
    return (cos_part, sign * sin_part)


def complex_apply(pattern, table_real, table_imag, real_part, imag_part):
    contract = partial(jnp.einsum, pattern, precision=lax.Precision.HIGHEST)
    return (
        contract(table_real, real_part) - contract(table_imag, imag_part),
        contract(table_real, imag_part) + contract(table_imag, real_part),
    )


def spectral_order(length):
    if length <= 256:
        return np.arange(length)
    outer_len = length // 128
    return (spectral_order(outer_len)[:, None] + outer_len * np.arange(128)[None, :]).reshape(-1)


def whole_forward(real_part, imag_part, length):
    if length <= 256:
        table_real, table_imag = dft_table(length, -1.0)
        return complex_apply("kn,...n->...k", table_real, table_imag, real_part, imag_part)
    inner_len = 128
    outer_len = length // inner_len
    lead = real_part.shape[:-1]
    real_part = jnp.swapaxes(real_part.reshape(lead + (outer_len, inner_len)), -1, -2)
    imag_part = jnp.swapaxes(imag_part.reshape(lead + (outer_len, inner_len)), -1, -2)
    real_part, imag_part = whole_forward(real_part, imag_part, outer_len)
    real_part = jnp.swapaxes(real_part, -1, -2)
    imag_part = jnp.swapaxes(imag_part, -1, -2)
    freq_idx = jnp.asarray(spectral_order(outer_len), dtype=jnp.int32)[:, None]
    inner_idx = jnp.arange(inner_len, dtype=jnp.int32)[None, :]
    cos_part, sin_part = twiddle(freq_idx * inner_idx, length)
    real_part, imag_part = rotate(real_part, imag_part, cos_part, -sin_part)
    table_real, table_imag = dft_table(inner_len, -1.0)
    real_part, imag_part = complex_apply(
        "ub,...tb->...tu", table_real, table_imag, real_part, imag_part
    )
    return (real_part.reshape(lead + (length,)), imag_part.reshape(lead + (length,)))


def whole_inverse(real_part, imag_part, length):
    if length <= 256:
        table_real, table_imag = dft_table(length, 1.0)
        return complex_apply("kn,...n->...k", table_real, table_imag, real_part, imag_part)
    inner_len = 128
    outer_len = length // inner_len
    lead = real_part.shape[:-1]
    real_part = real_part.reshape(lead + (outer_len, inner_len))
    imag_part = imag_part.reshape(lead + (outer_len, inner_len))
    table_real, table_imag = dft_table(inner_len, 1.0)
    real_part, imag_part = complex_apply(
        "bu,...tu->...tb", table_real, table_imag, real_part, imag_part
    )
    freq_idx = jnp.asarray(spectral_order(outer_len), dtype=jnp.int32)[:, None]
    inner_idx = jnp.arange(inner_len, dtype=jnp.int32)[None, :]
    cos_part, sin_part = twiddle(freq_idx * inner_idx, length)
    real_part, imag_part = rotate(real_part, imag_part, cos_part, sin_part)
    real_part, imag_part = whole_inverse(
        jnp.swapaxes(real_part, -1, -2), jnp.swapaxes(imag_part, -1, -2), outer_len
    )
    real_part = jnp.swapaxes(real_part, -1, -2)
    imag_part = jnp.swapaxes(imag_part, -1, -2)
    return (real_part.reshape(lead + (length,)), imag_part.reshape(lead + (length,)))


def owner_conv(stacked, groups, samples):
    chan_rows = stacked.shape[1]
    own_rows = chan_rows // groups
    span = groups * samples
    pieces = stacked.reshape(2, groups, own_rows, samples)
    rows_whole = lax.all_to_all(pieces, "seq", split_axis=1, concat_axis=3, tiled=True).reshape(
        2, own_rows, span
    )
    padded = jnp.concatenate([rows_whole, jnp.zeros_like(rows_whole)], axis=2)
    spec_real, spec_imag = whole_forward(padded, jnp.zeros_like(padded), 2 * span)
    prod_real = spec_real[0] * spec_real[1] - spec_imag[0] * spec_imag[1]
    prod_imag = spec_real[0] * spec_imag[1] + spec_imag[0] * spec_real[1]
    back_real, back_imag = whole_inverse(prod_real, prod_imag, 2 * span)
    conv_rows = back_real[:, :span]
    return lax.all_to_all(conv_rows, "seq", split_axis=1, concat_axis=0, tiled=True)


def per_device(signal, gating, response, skip_gain, mixing_weight):
    chan_rows, samples = signal.shape
    groups = lax.axis_size("seq")
    full_len = 2 * groups * samples
    stacked = jnp.stack([signal, response])
    conv = owner_conv(stacked, groups, samples)
    conv = conv / full_len
    mixed_in = gating * (conv + skip_gain[:, None] * signal)
    return lax.psum_scatter(
        jnp.dot(
            mixing_weight,
            mixed_in,
            precision=lax.Precision.HIGHEST,
            preferred_element_type=jnp.float32,
        ),
        "chan",
        scatter_dimension=0,
        tiled=True,
    )


def solution(mesh):
    in_specs = (P("chan", "seq"), P("chan", "seq"), P("chan", "seq"), P("chan"), P(None, "chan"))
    out_specs = P("chan", "seq")
    return jax.shard_map(
        per_device, mesh=mesh, in_specs=in_specs, out_specs=out_specs, check_vma=False
    )
```

profile of v0, /device:TPU:0, one launch (start us, length us, event | category | flops | bytes accessed | tf_op | source)
XLA Modules:
  0.0 486.4 jit_solution(6807660299492079792)
XLA Ops:
  6.5 0.0 copy-start
  6.5 4.6 pad_maximum_fusion
  11.1 0.0 copy-start.7
  11.1 7.4 %all-to-all-start = ((f32[2,8,8,8192]{3,2,0,1:T(8,128)}), f32[2,8,8,8192]{3,2,0,1:T(8,128)}, u32[]{:S(2)}, u32[]{:S(2)}) async-start(f32[2,8,8,8192]{3,2,0,1:T(8,128)} %pad_maximum_fusion), calls=%async_computation | async-start | bytes 8388608 | tf_op jit(solution)/shard_map/all_to_all | solution.py:97
  18.6 0.0 reduce-scatter.4.cloned.1.call-start
  18.6 0.1 sine_negate_fusion.1
  18.7 0.1 fusion.149
  18.7 0.0 copy-done.7
  18.7 2.1 fusion.70
  20.8 3.4 fusion.69
  24.3 8.9 %fusion.34 = f32[2,8,128,128,8]{3,4,2,1,0:T(8,128)} fusion(), kind=kOutput, calls=%fused_computation.58 | convolution fusion | flops 201327552 | bytes 8388608 | tf_op jit(solution)/shard_map/kn,...n->...k/dot_general | solution.py:32
  33.2 78.7 %all-to-all-done = f32[2,8,8,8192]{3,2,0,1:T(8,128)} async-done(((f32[2,8,8,8192]{3,2,0,1:T(8,128)}), f32[2,8,8,8192]{3,2,0,1:T(8,128)}, u32[]{:S(2)}, u32[]{:S(2)}) %all-to-all-start) | async-done | bytes 4194336 | tf_op jit(solution)/shard_map/all_to_all | solution.py:97
  111.8 6.6 %copy.47 = f32[2,1,8,8,8192]{4,3,2,0,1:T(8,128)} copy(f32[2,1,8,8,8192]{4,2,0,3,1:T(8,128)} %bitcast.3) | data formatting | bytes 8388608 | tf_op jit(solution)/shard_map/all_to_all | solution.py:97
  118.4 4.0 reshape.255
  122.4 2.7 pad_bitcast_fusion
  125.1 4.9 %copy.100 = f32[2,8,1024,128]{3,2,1,0:T(8,128)} copy(f32[2,8,1024,128]{3,1,2,0:T(8,128)S(1)} %pad_bitcast_fusion) | data formatting | bytes 16777216
  130.0 8.7 %copy.74 = f32[2,8,128,8,128]{4,3,2,1,0:T(8,128)} copy(f32[2,8,128,8,128]{2,4,3,1,0:T(8,128)} %bitcast.216) | data formatting | bytes 16777216 | tf_op jit(solution)/shard_map/reshape | solution.py:51
  138.6 12.5 %fusion.4 = f32[2,8,128,128,8]{3,4,2,1,0:T(8,128)} fusion(f32[2,8,128,8,128]{4,3,2,1,0:T(8,128)} %copy.74), kind=kOutput, calls=%fused_computation.14 | convolution fusion | flops 201327552 | bytes 16777216 | tf_op jit(solution)/shard_map/kn,...n->...k/dot_general | solution.py:33
  151.1 0.0 copy-done.1
  151.1 9.3 %fusion.6 = f32[2,8,128,128,8]{3,4,2,1,0:T(8,128)} fusion(f32[2,8,128,8,128]{4,3,2,1,0:T(8,128)S(1)} %copy-done.1), kind=kOutput, calls=%fused_computation.16 | convolution fusion | flops 201327488 | bytes 16777216 | tf_op jit(solution)/shard_map/kn,...n->...k/dot_general | solution.py:32
  160.4 15.3 %fusion.2 = (f32[2,8,128,8,128]{4,3,2,1,0:T(8,128)}, f32[2,8,128,8,128]{4,3,2,1,0:T(8,128)S(1)}) fusion(f32[8,128]{1,0:T(8,128)S(1)} %get-tuple-element.19, f32[8,128]{1,0:T(8,128)S(1)} %get-tuple-element.20, f32[2,8,128,128,8]{3,4,2,1,0:T(8,128)} %fusion.4, f32[2,8,128,128,8]{3,4,2,1,0:T(8,128)} %fusion.6, f32[2,8,128,128,8]{3,4,2,1,0:T(8,128)} %fusion.34), kind=kOutput, calls=%fused_computation.10 | convolution fusion | flops 218104704 | bytes 41951232 | tf_op jit(solution)/shard_map/kn,...n->...k/dot_general | solution.py:33
  175.7 11.1 %fusion.8 = f32[2,8,128,8,128]{2,4,3,1,0:T(8,128)} fusion(f32[2,8,128,8,128]{4,3,2,1,0:T(8,128)S(1)} %get-tuple-element.6), kind=kOutput, calls=%fused_computation.19 | convolution fusion | flops 3221454848 | bytes 16777216 | tf_op jit(solution)/shard_map/ub,...tb->...tu/dot_general | solution.py:33
  186.8 0.0 slice-start.1
  186.8 8.8 %fusion.10 = f32[2,8,128,8,128]{2,4,3,1,0:T(8,128)S(1)} fusion(f32[2,8,128,8,128]{4,3,2,1,0:T(8,128)S(1)} %get-tuple-element.6), kind=kOutput, calls=%fused_computation.21 | convolution fusion | flops 3221471232 | bytes 16777216 | tf_op jit(solution)/shard_map/ub,...tb->...tu/dot_general | solution.py:32
  195.7 0.0 slice-done
  195.7 0.0 slice-done.1
  195.7 13.0 %fusion.39 = f32[2,8,128,8,128]{2,4,3,1,0:T(8,128)} fusion(f32[2,8,128,8,128]{2,4,3,1,0:T(8,128)} %fusion.8, f32[2,8,128,8,128]{4,3,2,1,0:T(8,128)S(1)} %bitcast.211), kind=kOutput, calls=%fused_computation.61 | convolution fusion | flops 3223568384 | bytes 25165824 | tf_op jit(solution)/shard_map/ub,...tb->...tu/dot_general | solution.py:33
  208.7 10.7 %fusion.36 = f32[2,8,128,8,128]{2,4,3,1,0:T(8,128)} fusion(f32[2,8,128,8,128]{2,4,3,1,0:T(8,128)S(1)} %fusion.10, f32[2,8,128,8,128]{4,3,2,1,0:T(8,128)S(1)} %bitcast.211), kind=kOutput, calls=%fused_computation.60 | convolution fusion | flops 3223552000 | bytes 25165824 | tf_op jit(solution)/shard_map/ub,...tb->...tu/dot_general | solution.py:32
  219.4 7.0 %fusion = (f32[2,8,1024,128]{3,2,1,0:T(8,128)S(1)}, f32[2,8,1024,128]{3,2,1,0:T(8,128)S(1)}) fusion(f32[2,8,128,8,128]{2,4,3,1,0:T(8,128)} %fusion.36, f32[2,8,128,8,128]{2,4,3,1,0:T(8,128)} %fusion.39, f32[1024,128]{1,0:T(8,128)S(1)} %get-tuple-element.18, f32[1024,128]{1,0:T(8,128)S(1)} %get-tuple-element.17), kind=kLoop, calls=%fused_computation.4 | loop fusion | flops 12582912 | bytes 34603008 | tf_op jit(solution)/shard_map/sub | solution.py:18
  226.5 9.7 %fusion.88 = f32[2,8,1024,128]{3,2,1,0:T(8,128)} fusion(f32[2,8,1024,128]{3,2,1,0:T(8,128)S(1)} %get-tuple-element.7), kind=kOutput, calls=%fused_computation.116 | convolution fusion | flops 3221454848 | bytes 16777216 | tf_op jit(solution)/shard_map/ub,...tb->...tu/dot_general | solution.py:32
  236.2 7.8 %fusion.86 = f32[2,8,1024,128]{3,2,1,0:T(8,128)S(1)} fusion(f32[2,8,1024,128]{3,2,1,0:T(8,128)S(1)} %get-tuple-element.8), kind=kOutput, calls=%fused_computation.114 | convolution fusion | flops 3221454848 | bytes 16777216 | tf_op jit(solution)/shard_map/ub,...tb->...tu/dot_general | solution.py:33
  244.0 11.4 %convolution_subtract_fusion = f32[2,8,1024,128]{3,2,1,0:T(8,128)} fusion(f32[2,8,1024,128]{3,2,1,0:T(8,128)} %fusion.88, f32[2,8,1024,128]{3,2,1,0:T(8,128)S(1)} %get-tuple-element.8), kind=kOutput, calls=%fused_computation.63 | convolution fusion | flops 3223568384 | bytes 25165824 | tf_op jit(solution)/shard_map/ub,...tb->...tu/dot_general | solution.py:32
  255.4 9.5 %convolution_add_fusion = f32[2,8,1024,128]{3,2,1,0:T(8,128)} fusion(f32[2,8,1024,128]{3,2,1,0:T(8,128)S(1)} %fusion.86, f32[2,8,1024,128]{3,2,1,0:T(8,128)S(1)} %get-tuple-element.7), kind=kOutput, calls=%fused_computation.62 | convolution fusion | flops 3223568384 | bytes 25165824 | tf_op jit(solution)/shard_map/ub,...tb->...tu/dot_general | solution.py:33
  264.9 0.0 copy-done.2
  264.9 4.2 multiply_subtract_fusion
  269.1 3.8 fusion.22
  272.9 3.8 fusion.20
  276.8 0.0 copy-start.4
  276.8 0.0 copy-start.5
  276.8 3.8 fusion.44
  280.6 0.0 copy-done.4
  280.6 0.0 copy-done.5
  280.6 5.2 %fusion.18 = (f32[8,128,1024]{1,2,0:T(8,128)S(1)}, f32[8,128,1024]{1,2,0:T(8,128)S(1)}) fusion(f32[8,1024,128]{2,1,0:T(8,128)S(1)} %fusion.44, f32[128,1024]{0,1:T(8,128)S(1)} %copy-done.5, f32[128,1024]{0,1:T(8,128)S(1)} %copy-done.4, f32[8,1024,128]{2,1,0:T(8,128)S(1)} %fusion.20, f32[1,8,1024,128]{3,2,1,0:T(8,128)S(1)} %get-tuple-element.9), kind=kOutput, calls=%fused_computation.37 | convolution fusion | flops 1618182144 | bytes 22020096 | tf_op jit(solution)/shard_map/bu,...tu->...tb/dot_general | solution.py:33
  285.9 7.0 %fusion.84 = f32[8,128,8,128]{3,1,2,0:T(8,128)S(1)} fusion(f32[8,128,8,128]{1,3,2,0:T(8,128)S(1)} %bitcast.212), kind=kOutput, calls=%fused_computation.112 | convolution fusion | flops 1610842112 | bytes 8388608 | tf_op jit(solution)/shard_map/bu,...tu->...tb/dot_general | solution.py:32
  292.9 7.3 %fusion.82 = f32[8,128,8,128]{3,1,2,0:T(8,128)S(1)} fusion(f32[8,128,8,128]{1,3,2,0:T(8,128)S(1)} %bitcast.214), kind=kOutput, calls=%fused_computation.110 | convolution fusion | flops 1610842112 | bytes 8388608 | tf_op jit(solution)/shard_map/bu,...tu->...tb/dot_general | solution.py:33
  300.2 7.1 %convolution_subtract_fusion.1 = f32[8,128,8,128]{3,1,2,0:T(8,128)S(1)} fusion(f32[8,128,8,128]{3,1,2,0:T(8,128)S(1)} %fusion.84, f32[8,128,8,128]{1,3,2,0:T(8,128)S(1)} %bitcast.215), kind=kOutput, calls=%fused_computation.67 | convolution fusion | flops 1611890688 | bytes 12582912 | tf_op jit(solution)/shard_map/bu,...tu->...tb/dot_general | solution.py:32
  307.3 7.3 %fusion.16 = (f32[8,128,128,8]{2,1,3,0:T(8,128)S(1)}, f32[8,128,128,8]{2,1,3,0:T(8,128)S(1)}) fusion(f32[8,128,8,128]{3,1,2,0:T(8,128)S(1)} %convolution_subtract_fusion.1, f32[128,8]{0,1:T(8,128)S(1)} %get-tuple-element.21, f32[128,8]{0,1:T(8,128)S(1)} %get-tuple-element.22, f32[8,128,8,128]{3,1,2,0:T(8,128)S(1)} %fusion.82, ...), kind=kOutput, calls=%fused_computation.31 | convolution fusion | flops 1618182144 | bytes 20979712 | tf_op jit(solution)/shard_map/bu,...tu->...tb/dot_general | solution.py:33
  314.6 6.6 %fusion.28 = f32[8,128,128,8]{2,3,1,0:T(8,128)S(1)} fusion(f32[8,128,128,8]{2,1,3,0:T(8,128)S(1)} %get-tuple-element.14), kind=kOutput, calls=%fused_computation.49 | convolution fusion | flops 100664192 | bytes 8388608 | tf_op jit(solution)/shard_map/kn,...n->...k/dot_general | solution.py:32
  321.2 6.9 %subtract_bitcast_fusion = f32[8,128,8,128]{3,2,1,0:T(8,128)} fusion(f32[8,128,128,8]{2,3,1,0:T(8,128)S(1)} %fusion.28, f32[8,128,128,8]{2,1,3,0:T(8,128)S(1)} %get-tuple-element.13), kind=kOutput, calls=%fused_computation.53 | convolution fusion | flops 101712768 | bytes 12582912 | tf_op jit(solution)/shard_map/kn,...n->...k/dot_general | solution.py:32
  328.1 5.4 %copy.75 = f32[8,128,8,128]{1,3,2,0:T(8,128)} copy(f32[8,128,8,128]{3,2,1,0:T(8,128)} %subtract_bitcast_fusion) | data formatting | bytes 8388608 | tf_op jit(solution)/shard_map/reshape | solution.py:89
  333.5 4.6 copy.101
  338.1 0.0 copy-start.3
  338.1 0.0 copy-start.6
  338.1 0.0 copy-start.8
  338.1 0.1 slice.32
  338.3 52.3 %all_to_all.28 = f32[8,8,8192]{2,0,1:T(8,128)S(1)} all-to-all(f32[8,8,8192]{2,0,1:T(8,128)S(1)} %bitcast.219), channel_id=1, replica_groups=mesh['seq'=8,'chan'=4] {'seq'}, dimensions={1} | all-to-all | bytes 4194304 | tf_op jit(solution)/shard_map/all_to_all | solution.py:106
  390.6 0.0 copy-done
  390.6 0.0 copy-done.3
  390.6 0.0 copy-done.6
  390.6 0.0 copy-done.8
  390.6 9.1 %convolution_bitcast_fusion = f32[256,8192]{0,1:T(8,128)} fusion(f32[256,64]{0,1:T(8,128)S(1)} %copy-done, f32[64,8192]{1,0:T(8,128)S(1)} %copy-done.6, f32[64,8192]{1,0:T(8,128)S(1)} %copy-done.3, f32[8,8,8192]{2,0,1:T(8,128)S(1)} %all_to_all.28, f32[64]{0:T(128)S(1)} %copy-done.8), kind=kOutput, calls=%fused_computation | convolution fusion | flops 1612709888 | bytes 14745856 | tf_op jit(solution)/shard_map/dot_general | solution.py:118
  399.7 8.9 %copy.76 = f32[256,8192]{1,0:T(8,128)} copy(f32[256,8192]{0,1:T(8,128)} %convolution_bitcast_fusion) | data formatting | bytes 16777216
  408.6 0.0 reduce-scatter.4.cloned.1.call-update
  408.6 70.6 %reduce-scatter.4.cloned.1.call-done = f32[64,8192]{1,0:T(8,128)} async-done(((f32[256,8192]{1,0:T(8,128)}), f32[64,8192]{1,0:T(8,128)}) %reduce-scatter.4.cloned.1.call-update) | async-done | bytes 2097168 | tf_op jit(solution)/shard_map/reduce_scatter | solution.py:117
  (4 shorter events, 0.0 us)
Async XLA Ops:
  6.5 384.1 %copy-start = (f32[256,64]{0,1:T(8,128)S(1)}, f32[256,64]{0,1:T(8,128)}, u32[]{:S(2)}) copy-start(f32[256,64]{0,1:T(8,128)} %param.13) | copy-start | bytes 196612
  11.1 7.6 %copy-start.7 = (s32[1024]{0:T(1024)S(1)}, s32[1024]{0:T(1024)}, u32[]{:S(2)}) copy-start(s32[1024]{0:T(1024)} %constant.100.clone) | copy-start | bytes 12292
  11.1 100.7 %all-to-all-start = ((f32[2,8,8,8192]{3,2,0,1:T(8,128)}), f32[2,8,8,8192]{3,2,0,1:T(8,128)}, u32[]{:S(2)}, u32[]{:S(2)}) async-start(f32[2,8,8,8192]{3,2,0,1:T(8,128)} %pad_maximum_fusion), calls=%async_computation | async-start | bytes 8388608 | tf_op jit(solution)/shard_map/all_to_all | solution.py:97
  18.6 460.7 %reduce-scatter.4.cloned.1.call-start = ((), (), s32[]{:S(2)}) async-start(), calls=%async_computation.3 | async-start | bytes 10485760 | tf_op jit(solution)/shard_map/reduce_scatter | solution.py:117
  138.6 12.5 %copy-start.1 = (f32[2,8,128,8,128]{4,3,2,1,0:T(8,128)S(1)}, f32[2,8,128,8,128]{4,3,2,1,0:T(8,128)}, u32[]{:S(2)}) copy-start(f32[2,8,128,8,128]{4,3,2,1,0:T(8,128)} %copy.74) | copy-start | bytes 25165828
  175.7 20.0 %slice-start = ((s8[8388608]{0:T(1024)(128)(4,1)}), s8[4194304]{0:T(1024)(128)(4,1)S(1)}, s32[]{:S(2)}) async-start(s8[8388608]{0:T(1024)(128)(4,1)} %bitcast.210), calls=%async_computation.4 | async-start | bytes 8388608
  186.8 8.9 %slice-start.1 = ((s8[8388608]{0:T(1024)(128)(4,1)}), s8[4194304]{0:T(1024)(128)(4,1)S(1)}, s32[]{:S(2)}) async-start(s8[8388608]{0:T(1024)(128)(4,1)} %bitcast.210), calls=%async_computation.5 | async-start | bytes 8388608
  255.4 9.5 %copy-start.2 = (f32[2,8,1024,128]{3,2,1,0:T(8,128)S(1)}, f32[2,8,1024,128]{3,2,1,0:T(8,128)}, u32[]{:S(2)}) copy-start(f32[2,8,1024,128]{3,2,1,0:T(8,128)} %convolution_subtract_fusion) | copy-start | bytes 25165828
  276.8 3.9 copy-start.4
  276.8 3.9 copy-start.5
  338.1 52.5 %copy-start.3 = (f32[64,8192]{1,0:T(8,128)S(1)}, f32[64,8192]{1,0:T(8,128)}, u32[]{:S(2)}) copy-start(f32[64,8192]{1,0:T(8,128)} %param.9) | copy-start | bytes 6291460
  338.1 52.5 %copy-start.6 = (f32[64,8192]{1,0:T(8,128)S(1)}, f32[64,8192]{1,0:T(8,128)}, u32[]{:S(2)}) copy-start(f32[64,8192]{1,0:T(8,128)} %param.10) | copy-start | bytes 6291460
  338.1 52.5 %copy-start.8 = (f32[64]{0:T(128)S(1)}, f32[64]{0:T(128)}, u32[]{:S(2)}) copy-start(f32[64]{0:T(128)} %param.12) | copy-start | bytes 772
Sparse Core Ops, SparseCore 0:
  408.8 70.4 reduce-scatter.3
where the time goes:
time: 490 us; the launch traced here: 486 us
  matrix products  196 us (40%)
  waiting for transfers between devices  149 us (30%)
  blocking collectives  52.3 us (11%)
  local copies, waits for them, and re-layouts  45.9 us (9%)
  other arithmetic  21.5 us (4%)
  between operations  13.9 us (3%)
  starting transfers between devices  7.45 us (2%)
    all_to_all x1, waiting for transfers between devices, owner_conv(): lax.all_to_all(pieces, 'seq', split_axis=1, concat_axis=3, tiled=True)  78.7 us
    reduce_scatter x1, waiting for transfers between devices, per_device(): lax.psum_scatter(jnp.dot(mixing_weight, mixed_in, precision=lax.Precision...  70.6 us
    all_to_all x1, blocking collectives, owner_conv(): lax.all_to_all(conv_rows, 'seq', split_axis=1, concat_axis=0, tiled=True)  52.3 us
    dot_general x5, matrix products, complex_apply(): contract(table_imag, real_part)  47.6 us
    dot_general x6, matrix products, complex_apply(): contract(table_real, real_part) - contract(table_imag, imag_part)  47.5 us
    dot_general x6, matrix products, complex_apply(): contract(table_imag, imag_part)  46.6 us
    dot_general x5, matrix products, complex_apply(): contract(table_real, imag_part) + contract(table_imag, real_part)  45.3 us
    unnamed x26, local copies, waits for them, and re-layouts  21.2 us
  transfers between devices with their start and end apart: 2, of which 2 were waited for; matrix products, arithmetic and copies ran while one was open for 3% of the time, Pallas kernels for 0%

commit v1 on v0

v1 whole, which is shorter than its diff:
```python
from functools import partial
import math

import jax
import jax.numpy as jnp
import numpy as np
from jax import lax
from jax.experimental import pallas as pl
from jax.experimental.pallas import tpu as pltpu
from jax.sharding import PartitionSpec as P

INNER = 256


def halves(table):
    high = np.asarray(table, np.float32).astype(jnp.bfloat16)
    low = (np.asarray(table, np.float64) - high.astype(np.float64)).astype(np.float32).astype(jnp.bfloat16)
    return high, low


def split(value):
    high = value.astype(jnp.bfloat16)
    return high, (value - high.astype(jnp.float32)).astype(jnp.bfloat16)


def tables(span):
    outer = span // INNER
    step_out = np.arange(outer, dtype=np.float64)
    step_in = np.arange(INNER, dtype=np.float64)
    angle = 2 * np.pi * np.mod((4 * step_out[:, None] + 1) * step_out[None, :], 4 * outer) / (4 * outer)
    cos_out, sin_out = np.cos(angle), -np.sin(angle)
    high, low = halves(np.concatenate([cos_out, sin_out], axis=0))
    first = np.concatenate([high, high, low], axis=1)
    angle = 2 * np.pi * np.mod((4 * step_out[:, None] + 1) * step_in[None, :], 4 * span) / (4 * span)
    twiddle = np.stack([np.cos(angle), -np.sin(angle)]).astype(np.float32)
    angle = 2 * np.pi * np.mod(step_in[:, None] * step_in[None, :], INNER) / INNER
    cos_in, sin_in = np.cos(angle), -np.sin(angle)
    high, low = halves(np.block([[cos_in, sin_in], [-sin_in, cos_in]]))
    second = np.concatenate([high, high, low], axis=0)
    high, low = halves(np.block([[cos_in, -sin_in], [sin_in, cos_in]]))
    third = np.concatenate([high, high, low], axis=0)
    high, low = halves(np.concatenate([cos_out.T, sin_out.T], axis=1) / span)
    fourth = np.concatenate([high, high, low], axis=1)
    return first, twiddle, second, third, fourth


def matmul(left, right):
    return jnp.dot(left, right, preferred_element_type=jnp.float32)


def conv_row(signal, response, first, twiddle, second, third, fourth):
    outer = signal.shape[0]
    high, low = split(jnp.concatenate([signal, response], axis=1))
    mid = matmul(first[...], jnp.concatenate([high, low, high], axis=0))
    tw_real, tw_imag = twiddle[0], twiddle[1]
    spectra = []
    for place in range(2):
        cols = slice(place * INNER, (place + 1) * INNER)
        real, imag = mid[:outer, cols], mid[outer:, cols]
        turned = jnp.concatenate(
            [real * tw_real - imag * tw_imag, real * tw_imag + imag * tw_real], axis=1
        )
        high, low = split(turned)
        spectra.append(matmul(jnp.concatenate([high, low, high], axis=1), second[...]))
    s_real, s_imag = spectra[0][:, :INNER], spectra[0][:, INNER:]
    r_real, r_imag = spectra[1][:, :INNER], spectra[1][:, INNER:]
    prod = jnp.concatenate(
        [s_real * r_real - s_imag * r_imag, s_real * r_imag + s_imag * r_real], axis=1
    )
    high, low = split(prod)
    back = matmul(jnp.concatenate([high, low, high], axis=1), third[...])
    real, imag = back[:, :INNER], back[:, INNER:]
    turned = jnp.concatenate(
        [real * tw_real + imag * tw_imag, imag * tw_real - real * tw_imag], axis=0
    )
    high, low = split(turned)
    return matmul(fourth[...], jnp.concatenate([high, low, high], axis=0))


def conv_kernel(rows_ref, first, twiddle, second, third, fourth, out_ref):
    out_ref[0] = conv_row(rows_ref[0, 0], rows_ref[1, 0], first, twiddle, second, third, fourth)


def conv_call(rows):
    own_rows, outer, inner = rows.shape[1:]
    consts = [jnp.asarray(t) for t in tables(outer * inner)]
    whole = pl.BlockSpec(memory_space=pltpu.VMEM)
    return pl.pallas_call(
        conv_kernel,
        grid=(own_rows,),
        in_specs=[pl.BlockSpec((2, 1, outer, inner), lambda r: (0, r, 0, 0))] + [whole] * 5,
        out_specs=pl.BlockSpec((1, outer, inner), lambda r: (r, 0, 0)),
        out_shape=jax.ShapeDtypeStruct((own_rows, outer, inner), jnp.float32),
        compiler_params=pltpu.CompilerParams(vmem_limit_bytes=60 * 2**20),
        name="conv",
    )(rows, *consts)


def per_device(signal, gating, response, skip_gain, mixing_weight):
    chan_rows, samples = signal.shape
    groups = lax.axis_size("seq")
    own_rows = chan_rows // groups
    outer = groups * samples // INNER
    stacked = jnp.stack([signal, response]).reshape(2, groups, own_rows, samples // INNER, INNER)
    rows = lax.all_to_all(stacked, "seq", split_axis=1, concat_axis=3, tiled=True)
    conv = conv_call(rows.reshape(2, own_rows, outer, INNER))
    conv = lax.all_to_all(
        conv.reshape(own_rows, groups, samples // INNER, INNER), "seq", split_axis=1, concat_axis=0, tiled=True
    ).reshape(chan_rows, samples)
    mixed_in = gating * (conv + skip_gain[:, None] * signal)
    return lax.psum_scatter(
        jnp.dot(
            mixing_weight,
            mixed_in,
            precision=lax.Precision.HIGHEST,
            preferred_element_type=jnp.float32,
        ),
        "chan",
        scatter_dimension=0,
        tiled=True,
    )


def solution(mesh):
    in_specs = (P("chan", "seq"), P("chan", "seq"), P("chan", "seq"), P("chan"), P(None, "chan"))
    out_specs = P("chan", "seq")
    return jax.shard_map(
        per_device, mesh=mesh, in_specs=in_specs, out_specs=out_specs, check_vma=False
    )
```

time: 490 us -> 289 us (0.59)
  matrix products: 196 us -> 9.05 us
  blocking collectives: 52.3 us -> 152 us
  waiting for transfers between devices: 149 us -> 70.5 us
  local copies, waits for them, and re-layouts: 45.9 us -> 18.7 us
  Pallas kernels: 0 us -> 25 us
  other arithmetic: 21.5 us -> 0.58 us
  starting transfers between devices: 7.45 us -> 0.01 us
    dot_general x22 -> x0, matrix products: 187 us -> none  [the longest x5 47.6 us: complex_apply(): contract(table_imag, real_part)]
    all_to_all x1 -> x2, blocking collectives: 52.3 us -> 152 us  [the longest x1 100 us: per_device(): lax.all_to_all(stacked, 'seq', split_axis=1, concat_axis=3, tiled=True)]
    all_to_all x1 -> x0, waiting for transfers between devices: 78.7 us -> none  [owner_conv(): lax.all_to_all(pieces, 'seq', split_axis=1, concat_axis=3, tiled=True)]
    pallas_call x0 -> x1, Pallas kernels: none -> 25 us  [conv_call(): pl.pallas_call(conv_kernel, grid=(own_rows,), in_specs=[pl.BlockSpec((2,...]
    reshape x3 -> x1, local copies, waits for them, and re-layouts: 18 us -> 1.73 us  [per_device(): conv.reshape(own_rows, groups, samples // INNER, INNER)]
    sub x2 -> x0, other arithmetic: 11.2 us -> none  [the longest x1 7.05 us: rotate(): real_part * cos_part - imag_part * sin_part]
    unnamed x26 -> x10, local copies, waits for them, and re-layouts: 21.2 us -> 11.2 us
    all_to_all x1 -> x0, starting transfers between devices: 7.41 us -> none  [owner_conv(): lax.all_to_all(pieces, 'seq', split_axis=1, concat_axis=3, tiled=True)]
  transfers between devices with their start and end apart: 2 -> 1, of which waited for: 2 -> 1; matrix products, arithmetic and copies ran while one was open for 3% -> 0% of each run, Pallas kernels for 0% -> 0%
where the time goes in v1:
time: 289 us
  blocking collectives  152 us (53%)
  waiting for transfers between devices  70.5 us (24%)
  Pallas kernels  25 us (9%)
  local copies, waits for them, and re-layouts  18.7 us (6%)
  between operations  13.4 us (5%)
  matrix products  9.05 us (3%)
    all_to_all x1, blocking collectives, per_device(): lax.all_to_all(stacked, 'seq', split_axis=1, concat_axis=3, tiled=True)  100 us
    reduce_scatter x1, waiting for transfers between devices, per_device(): lax.psum_scatter(jnp.dot(mixing_weight, mixed_in, precision=lax.Precision...  70.5 us
    all_to_all x1, blocking collectives, per_device(): lax.all_to_all(conv.reshape(own_rows, groups, samples // INNER, INNER), '...  51.4 us
    pallas_call x1, Pallas kernels, conv_call(): pl.pallas_call(conv_kernel, grid=(own_rows,), in_specs=[pl.BlockSpec((2,...  25 us
    unnamed x10, local copies, waits for them, and re-layouts  11.2 us
    dot_general x1, matrix products, per_device(): jnp.dot(mixing_weight, mixed_in, precision=lax.Precision.HIGHEST, preferr...  9.05 us
  transfers between devices with their start and end apart: 1, of which 1 were waited for; matrix products, arithmetic and copies ran while one was open for 0% of the time, Pallas kernels for 0%

profile of v1, /device:TPU:0, one launch (start us, length us, event | category | flops | bytes accessed | tf_op | source)
XLA Modules:
  0.0 288.9 jit_solution(17521715110210027831)
XLA Ops:
  6.5 0.0 copy-start
  6.5 0.0 reduce-scatter.4.cloned.1.call-start
  6.5 3.6 %copy_bitcast_fusion = (f32[1,8,8,32,256]{4,3,2,0,1:T(8,128)S(1)}, f32[1,8,8,32,256]{4,3,2,0,1:T(8,128)S(1)}) fusion(f32[8,8,32,256]{3,1,2,0:T(8,128)} %bitcast.32, f32[8,8,32,256]{3,1,2,0:T(8,128)} %bitcast.31), kind=kLoop, calls=%fused_computation.2 | loop fusion | bytes 8388608 | tf_op jit(solution)/shard_map/stack | solution.py:104
  10.1 0.6 pad_maximum_fusion
  10.7 100.3 %all_to_all.30 = f32[2,8,8,32,256]{4,3,2,0,1:T(8,128)S(1)} all-to-all(f32[2,8,8,32,256]{4,3,2,0,1:T(8,128)S(1)} %pad_maximum_fusion), channel_id=1, replica_groups=mesh['seq'=8,'chan'=4] {'seq'}, dimensions={1} | all-to-all | bytes 8388608 | tf_op jit(solution)/shard_map/all_to_all | solution.py:105
  111.0 2.3 copy.15
  113.2 25.0 %conv.1 = f32[8,256,256]{2,1,0:T(8,128)} custom-call(f32[2,8,256,256]{3,2,1,0:T(8,128)} %bitcast.27, bf16[512,768]{1,0:T(8,128)(2,1)} %constant.10.clone.first, f32[2,256,256]{2,1,0:T(8,128)} %constant.11.clone.twiddle, bf16[1536,512]{1,0:T(8,128)(2,1)} %constant.12.clone.second, bf16[1536,512]{1,0:T(8,128)(2,1)} %constant.13.clone.third, ...), custom_call_target="tpu_custom_call" | custom-call | tf_op jit(solution)/shard_map/conv/pallas_call | solution.py:88
  138.2 1.7 copy.16
  139.9 51.4 %all_to_all.31 = f32[8,8,32,256]{3,2,0,1:T(8,128)S(1)} all-to-all(f32[8,8,32,256]{3,2,0,1:T(8,128)S(1)} %copy.16), channel_id=1, replica_groups=mesh['seq'=8,'chan'=4] {'seq'}, dimensions={1} | all-to-all | bytes 4194304 | tf_op jit(solution)/shard_map/all_to_all | solution.py:107
  191.3 0.0 copy-start.1
  191.3 0.0 copy-start.2
  191.3 0.0 copy-start.3
  191.3 1.2 copy.22
  192.5 0.0 copy-done
  192.5 0.4 copy-done.1
  192.9 0.6 copy-done.2
  193.5 0.0 copy-done.3
  193.5 9.1 %convolution_bitcast_fusion = f32[256,8192]{0,1:T(8,128)} fusion(f32[256,64]{0,1:T(8,128)S(1)} %copy-done, f32[64,8192]{1,0:T(8,128)S(1)} %copy-done.2, f32[64,8192]{1,0:T(8,128)S(1)} %bitcast.30, f32[64,8192]{1,0:T(8,128)S(1)} %copy-done.1, f32[64]{0:T(128)S(1)} %copy-done.3), kind=kOutput, calls=%fused_computation | convolution fusion | flops 1612185600 | bytes 14745856 | tf_op jit(solution)/shard_map/dot_general | solution.py:112
  202.6 8.9 %copy.18 = f32[256,8192]{1,0:T(8,128)} copy(f32[256,8192]{0,1:T(8,128)} %convolution_bitcast_fusion) | data formatting | bytes 16777216
  211.5 0.0 reduce-scatter.4.cloned.1.call-update
  211.5 70.5 %reduce-scatter.4.cloned.1.call-done = f32[64,8192]{1,0:T(8,128)} async-done(((f32[256,8192]{1,0:T(8,128)}), f32[64,8192]{1,0:T(8,128)}) %reduce-scatter.4.cloned.1.call-update) | async-done | bytes 2097168 | tf_op jit(solution)/shard_map/reduce_scatter | solution.py:111
Async XLA Ops:
  6.5 186.0 %copy-start = (f32[256,64]{0,1:T(8,128)S(1)}, f32[256,64]{0,1:T(8,128)}, u32[]{:S(2)}) copy-start(f32[256,64]{0,1:T(8,128)} %param.14) | copy-start | bytes 196612
  6.5 275.5 %reduce-scatter.4.cloned.1.call-start = ((), (), s32[]{:S(2)}) async-start(), calls=%async_computation.3 | async-start | bytes 10485760 | tf_op jit(solution)/shard_map/reduce_scatter | solution.py:111
  191.3 1.6 copy-start.1
  191.3 2.2 copy-start.2
  191.3 2.2 copy-start.3
Sparse Core Ops, SparseCore 0:
  211.6 70.3 reduce-scatter.3

commit v2 on v1

v2 whole, which is shorter than its diff:
```python
from functools import partial
import math

import jax
import jax.numpy as jnp
import numpy as np
from jax import lax
from jax.experimental import pallas as pl
from jax.experimental.pallas import tpu as pltpu
from jax.sharding import PartitionSpec as P

INNER = 256


def halves(table):
    high = np.asarray(table, np.float32).astype(jnp.bfloat16)
    low = (np.asarray(table, np.float64) - high.astype(np.float64)).astype(np.float32).astype(jnp.bfloat16)
    return high, low


def split(value):
    high = value.astype(jnp.bfloat16)
    return high, (value - high.astype(jnp.float32)).astype(jnp.bfloat16)


def tables(span):
    outer = span // INNER
    step_out = np.arange(outer, dtype=np.float64)
    step_in = np.arange(INNER, dtype=np.float64)
    angle = 2 * np.pi * np.mod((4 * step_out[:, None] + 1) * step_out[None, :], 4 * outer) / (4 * outer)
    cos_out, sin_out = np.cos(angle), -np.sin(angle)
    first = np.concatenate(halves(np.concatenate([cos_out, sin_out], axis=0)), axis=1)
    angle = 2 * np.pi * np.mod((4 * step_out[:, None] + 1) * step_in[None, :], 4 * span) / (4 * span)
    twiddle = np.stack([np.cos(angle), -np.sin(angle)]).astype(np.float32)
    angle = 2 * np.pi * np.mod(step_in[:, None] * step_in[None, :], INNER) / INNER
    cos_in, sin_in = np.cos(angle), -np.sin(angle)
    second = np.concatenate(halves(np.block([[cos_in, sin_in], [-sin_in, cos_in]])), axis=0)
    last = np.concatenate(halves(np.concatenate([cos_out.T, -sin_out.T], axis=1) / span), axis=1)
    return first, twiddle, second, last


def matmul(left, right):
    return jnp.dot(left, right, preferred_element_type=jnp.float32)


def table_left(table, value):
    high, low = split(value)
    depth = value.shape[0]
    return matmul(table[...], jnp.concatenate([high, high], axis=0)) + matmul(table[:, :depth], low)


def table_right(value, table):
    high, low = split(value)
    depth = value.shape[1]
    return matmul(jnp.concatenate([high, high], axis=1), table[...]) + matmul(low, table[:depth, :])


def conv_row(signal, response, first, twiddle, second, last):
    outer = signal.shape[0]
    mid = table_left(first, jnp.concatenate([signal, response], axis=1))
    tw_real, tw_imag = twiddle[0], twiddle[1]
    turned = []
    for place in range(2):
        cols = slice(place * INNER, (place + 1) * INNER)
        real, imag = mid[:outer, cols], mid[outer:, cols]
        turned.append(jnp.concatenate(
            [real * tw_real - imag * tw_imag, real * tw_imag + imag * tw_real], axis=1
        ))
    spectra = table_right(jnp.concatenate(turned, axis=0), second)
    s_real, s_imag = spectra[:outer, :INNER], spectra[:outer, INNER:]
    r_real, r_imag = spectra[outer:, :INNER], spectra[outer:, INNER:]
    prod = jnp.concatenate(
        [s_real * r_real - s_imag * r_imag, -(s_real * r_imag + s_imag * r_real)], axis=1
    )
    back = table_right(prod, second)
    real, imag = back[:, :INNER], back[:, INNER:]
    turned = jnp.concatenate(
        [real * tw_real - imag * tw_imag, imag * tw_real + real * tw_imag], axis=0
    )
    return table_left(last, turned)


MESH_ID = pl.DeviceIdType.MESH


def layer_kernel(
    groups, own_rows, chans, signal, response, gating, skip, weight,
    first, twiddle, second, last, out,
    send, held, made, conv, mixed, wbuf,
    fwd_send, fwd_recv, back_send, back_recv, own_sem, row_send, row_recv, w_send, w_recv, sib_sem, sib_recv, rel_send, rel_recv,
):
    chan_rows = groups * own_rows
    samples = signal.shape[0] * 128 // chan_rows
    pieces = samples // INNER
    chips = chans // 2
    me = lax.axis_index("seq")
    mine = lax.axis_index("chan")
    chip, core = mine // 2, mine % 2
    sibling = chip * 2 + 1 - core
    out_rows = out.shape[0]

    barrier = pltpu.get_barrier_semaphore()
    for off in range(1, groups):
        pl.semaphore_signal(barrier, inc=1, device_id={"seq": lax.rem(me + off, groups)}, device_id_type=MESH_ID)
    for off in range(1, chans):
        pl.semaphore_signal(barrier, inc=1, device_id={"chan": lax.rem(mine + off, chans)}, device_id_type=MESH_ID)
    pl.semaphore_wait(barrier, groups + chans - 2)

    def native(ref, row, half):
        start = (row // 8) * (samples // 128 * 8) + lax.rem(row, 8) + 8 * half
        return ref[pl.ds(start, pieces, stride=16), :]

    def forward(j, off):
        peer = lax.rem(me + off, groups)
        return pltpu.make_async_remote_copy(
            send.at[j, peer], held.at[j, me], fwd_send.at[j, off - 1], fwd_recv.at[j, off - 1],
            device_id={"seq": peer}, device_id_type=MESH_ID)

    def backward(j, off):
        peer = lax.rem(me + off, groups)
        return pltpu.make_async_remote_copy(
            made.at[j, peer], conv.at[j, me], back_send.at[j, off - 1], back_recv.at[j, off - 1],
            device_id={"seq": peer}, device_id_type=MESH_ID)

    def own_in(j):
        return pltpu.make_async_copy(send.at[j, me], held.at[j, me], own_sem.at[0, j])

    def own_back(j):
        return pltpu.make_async_copy(made.at[j, me], conv.at[j, me], own_sem.at[1, j])

    block = groups * pieces

    def chunk(who, j):
        return mixed.at[:, pl.ds(pl.multiple_of((who * own_rows + j) * block, block), block), :]

    def to_sibling(j):
        return pltpu.make_async_remote_copy(
            chunk(mine, j), chunk(mine, j), sib_sem.at[j], sib_recv.at[j],
            device_id={"chan": sibling}, device_id_type=MESH_ID)

    def to_chip(j, off):
        return pltpu.make_async_remote_copy(
            chunk(mine, j), chunk(mine, j), row_send.at[j, off - 1], row_recv.at[j, off - 1],
            device_id={"chan": lax.rem(chip + off, chips) * 2 + core}, device_id_type=MESH_ID)

    def relay(j, off):
        who = lax.rem(chip + chips - off, chips) * 2 + core
        return pltpu.make_async_remote_copy(
            chunk(who, j), chunk(who, j), rel_send.at[j, off - 1], rel_recv.at[j, off - 1],
            device_id={"chan": sibling}, device_id_type=MESH_ID)

    def weights(off):
        peer = lax.rem(mine + off, chans)
        return pltpu.make_async_remote_copy(
            weight.at[pl.ds(pl.multiple_of(peer * out_rows, 8), out_rows), :], wbuf.at[off - 1],
            w_send.at[off - 1], w_recv.at[off - 1],
            device_id={"chan": peer}, device_id_type=MESH_ID)

    @pl.loop(0, own_rows)
    def _(j):
        for g in range(groups):
            for place, ref in enumerate((signal, response)):
                for half in range(2):
                    send[j, g, place, :, half * 128:(half + 1) * 128] = native(ref, g * own_rows + j, half)
        for off in range(1, groups):
            forward(j, off).start()
        own_in(j).start()

    for off in range(1, chans):
        weights(off).start()

    @pl.loop(0, own_rows)
    def _(j):
        own_in(j).wait()
        for off in range(1, groups):
            forward(j, off).wait_recv()
        rows = held[j]
        made[j] = conv_row(
            rows[:, 0].reshape(groups * pieces, INNER), rows[:, 1].reshape(groups * pieces, INNER),
            first, twiddle, second, last,
        ).reshape(groups, pieces, INNER)
        for off in range(1, groups):
            backward(j, off).start()
        own_back(j).start()

    def pass_on(j):
        for off in range(1, chips):
            to_chip(j, off).wait_recv()
            relay(j, off).start()

    @pl.loop(0, own_rows)
    def _(j):
        own_back(j).wait()
        for off in range(1, groups):
            backward(j, off).wait_recv()
        for g in range(groups):
            row = g * own_rows + j
            gain = skip[j, g:g + 1, :]
            for half in range(2):
                lanes = slice(half * 128, (half + 1) * 128)
                start = pl.multiple_of((mine * own_rows + j) * block + g * pieces, pieces)
                mixed[half, pl.ds(start, pieces), :] = native(gating, row, half) * (
                    conv[j, g, :, lanes] + gain * native(signal, row, half)
                )
        to_sibling(j).start()
        for off in range(1, chips):
            to_chip(j, off).start()

        @pl.when(j > 0)
        def _():
            pass_on(j - 1)

    pass_on(own_rows - 1)

    total = weight[pl.ds(pl.multiple_of(mine * out_rows, 8), out_rows), :]
    for off in range(1, chans):
        weights(off).wait()
        total = total + wbuf[off - 1]
    w_high, w_low = split(total)

    @pl.loop(0, own_rows)
    def _(j):
        for off in range(1, groups):
            forward(j, off).wait_send()
            backward(j, off).wait_send()
        to_sibling(j).wait()
        for off in range(1, chips):
            to_chip(j, off).wait_send()
            relay(j, off).wait()

    depth = chans * chan_rows

    @pl.loop(0, pieces)
    def _(i):
        for half in range(2):
            high, low = split(mixed[half, pl.ds(i, depth, stride=pieces), :])
            out[:, pl.ds(pl.multiple_of(i * INNER + half * 128, 128), 128)] = (
                matmul(w_high, high) + matmul(w_high, low) + matmul(w_low, high)
            )


def tiles(value):
    rows, columns = value.shape
    return value.reshape(rows // 8, 8, columns // 128, 128).transpose(0, 2, 1, 3).reshape(-1, 128)


def per_device(signal, gating, response, skip_gain, mixing_weight):
    chan_rows, samples = signal.shape
    groups = lax.axis_size("seq")
    chans = lax.axis_size("chan")
    own_rows = chan_rows // groups
    pieces = samples // INNER
    chips = chans // 2
    depth = mixing_weight.shape[0]
    out_rows = depth // chans
    consts = [jnp.asarray(t) for t in tables(groups * samples)]
    skip = jnp.broadcast_to(skip_gain.reshape(groups, own_rows).T[:, :, None], (own_rows, groups, 128))
    turned = mixing_weight.reshape(depth, groups, own_rows).swapaxes(1, 2).reshape(depth, chan_rows)
    weight = lax.dynamic_update_slice(
        jnp.zeros((depth, chans * chan_rows), jnp.float32), turned, (0, lax.axis_index("chan") * chan_rows)
    )
    whole = pl.BlockSpec(memory_space=pltpu.VMEM)
    f32 = jnp.float32
    sems = pltpu.SemaphoreType.DMA
    rows = chans * chan_rows * pieces
    return pl.pallas_call(
        partial(layer_kernel, groups, own_rows, chans),
        in_specs=[whole] * 9,
        out_specs=whole,
        out_shape=jax.ShapeDtypeStruct((out_rows, samples), f32),
        scratch_shapes=[
            pltpu.VMEM((own_rows, groups, 2, pieces, INNER), f32),
            pltpu.VMEM((own_rows, groups, 2, pieces, INNER), f32),
            pltpu.VMEM((own_rows, groups, pieces, INNER), f32),
            pltpu.VMEM((own_rows, groups, pieces, INNER), f32),
            pltpu.VMEM((2, rows, 128), f32),
            pltpu.VMEM((chans - 1, out_rows, chans * chan_rows), f32),
            sems((own_rows, groups - 1)), sems((own_rows, groups - 1)),
            sems((own_rows, groups - 1)), sems((own_rows, groups - 1)),
            sems((2, own_rows)),
            sems((own_rows, chips - 1)), sems((own_rows, chips - 1)),
            sems((chans - 1,)), sems((chans - 1,)),
            sems((own_rows,)), sems((own_rows,)),
            sems((own_rows, chips - 1)), sems((own_rows, chips - 1)),
        ],
        compiler_params=pltpu.CompilerParams(
            collective_id=0, has_side_effects=True, vmem_limit_bytes=62 * 2**20
        ),
        name="layer",
    )(tiles(signal), tiles(response), tiles(gating), skip, weight, *consts)


def solution(mesh):
    in_specs = (P("chan", "seq"), P("chan", "seq"), P("chan", "seq"), P("chan"), P(None, "chan"))
    out_specs = P("chan", "seq")
    return jax.shard_map(
        per_device, mesh=mesh, in_specs=in_specs, out_specs=out_specs, check_vma=False
    )
```

time: 289 us -> 197 us (0.68)
  Pallas kernels: 25 us -> 188 us
  blocking collectives: 152 us -> 0 us
  waiting for transfers between devices: 70.5 us -> 0 us
  between operations: 13.4 us -> 0.04 us
  local copies, waits for them, and re-layouts: 18.7 us -> 7.31 us
  matrix products: 9.05 us -> 0 us
    pallas_call x1, Pallas kernels: 25 us -> 188 us  [per_device(): pl.pallas_call(partial(layer_kernel, groups, own_rows, chans), in_specs=[...]
    all_to_all x2 -> x0, blocking collectives: 152 us -> none  [the longest x1 100 us: per_device(): lax.all_to_all(stacked, 'seq', split_axis=1, concat_axis=3, tiled=True)]
    reduce_scatter x1 -> x0, waiting for transfers between devices: 70.5 us -> none  [per_device(): lax.psum_scatter(jnp.dot(mixing_weight, mixed_in, precision=lax.Precision...]
    dot_general x1 -> x0, matrix products: 9.05 us -> none  [per_device(): jnp.dot(mixing_weight, mixed_in, precision=lax.Precision.HIGHEST, preferr...]
    unnamed x10 -> x3, local copies, waits for them, and re-layouts: 11.2 us -> 3.76 us
    another operation x1 -> x0, local copies, waits for them, and re-layouts: 3.57 us -> none  [per_device(): jnp.stack([signal, response])]
  transfers between devices with their start and end apart: 1 -> 0, of which waited for: 1 -> 0; matrix products, arithmetic and copies ran while one was open for 0% -> 0% of each run, Pallas kernels for 0% -> 0%
where the time goes in v2:
time: 197 us; the launch traced here: 195 us
  Pallas kernels  188 us (95%)
  local copies, waits for them, and re-layouts  7.31 us (4%)
    pallas_call x1, Pallas kernels, per_device(): pl.pallas_call(partial(layer_kernel, groups, own_rows, chans), in_specs=[...  188 us

profile of v2, /device:TPU:0, one launch (start us, length us, event | category | flops | bytes accessed | tf_op | source)
XLA Modules:
  0.0 195.4 jit_solution(17843636831063363164)
XLA Ops:
  0.0 0.7 reshape.34
  0.7 0.1 copy.14
  0.8 0.7 broadcast_in_dim.4.skip
  1.5 0.9 copy.18
  2.4 0.1 copy.16
  2.5 1.1 dynamic_update_slice.3.weight
  3.6 0.0 copy-start
  3.6 0.7 copy-done
  4.3 188.1 %layer.1 = f32[64,8192]{1,0:T(8,128)} custom-call(f32[4096,128]{1,0:T(8,128)} %bitcast.22, f32[4096,128]{1,0:T(8,128)} %bitcast.23, f32[4096,128]{1,0:T(8,128)} %bitcast.24, f32[8,8,128]{2,1,0:T(8,128)} %broadcast_in_dim.4.skip, f32[256,256]{1,0:T(8,128)} %copy-done, bf16[512,512]{1,0:T(8,128)(2,1)} %constant.20.clone.first, ...), custom_call_target="tpu_custom_call" | custom-call | tf_op jit(solution)/shard_map/layer/pallas_call | solution.py:266
  192.3 3.1 %copy.21 = f32[64,8192]{1,0:T(8,128)} copy(f32[64,8192]{1,0:T(8,128)} %layer.1) | data formatting | bytes 4194304
  (1 shorter events, 0.0 us)
Async XLA Ops:
  3.6 0.7 copy-start

commit v3 on v2

v3 whole, which is shorter than its diff:
```python
from functools import partial
import math

import jax
import jax.numpy as jnp
import numpy as np
from jax import lax
from jax.experimental import pallas as pl
from jax.experimental.pallas import tpu as pltpu
from jax.sharding import PartitionSpec as P

INNER = 256


def halves(table):
    high = np.asarray(table, np.float32).astype(jnp.bfloat16)
    low = (np.asarray(table, np.float64) - high.astype(np.float64)).astype(np.float32).astype(jnp.bfloat16)
    return high, low


def split(value):
    high = value.astype(jnp.bfloat16)
    return high, (value - high.astype(jnp.float32)).astype(jnp.bfloat16)


def tables(span):
    outer = span // INNER
    step_out = np.arange(outer, dtype=np.float64)
    step_in = np.arange(INNER, dtype=np.float64)
    angle = 2 * np.pi * np.mod((4 * step_out[:, None] + 1) * step_out[None, :], 4 * outer) / (4 * outer)
    cos_out, sin_out = np.cos(angle), -np.sin(angle)
    first = np.concatenate(halves(np.concatenate([cos_out, sin_out], axis=0)), axis=1)
    angle = 2 * np.pi * np.mod((4 * step_out[:, None] + 1) * step_in[None, :], 4 * span) / (4 * span)
    twiddle = np.stack([np.cos(angle), -np.sin(angle)]).astype(np.float32)
    angle = 2 * np.pi * np.mod(step_in[:, None] * step_in[None, :], INNER) / INNER
    cos_in, sin_in = np.cos(angle), -np.sin(angle)
    second = np.concatenate(halves(np.block([[cos_in, sin_in], [-sin_in, cos_in]])), axis=0)
    last = np.concatenate(halves(np.concatenate([cos_out.T, -sin_out.T], axis=1) / span), axis=1)
    return first, twiddle, second, last


def matmul(left, right):
    return jnp.dot(left, right, preferred_element_type=jnp.float32)


def table_left(table, value):
    high, low = split(value)
    depth = value.shape[0]
    return matmul(table[...], jnp.concatenate([high, high], axis=0)) + matmul(table[:, :depth], low)


def table_right(value, table):
    high, low = split(value)
    depth = value.shape[1]
    return matmul(jnp.concatenate([high, high], axis=1), table[...]) + matmul(low, table[:depth, :])


def conv_row(signal, response, first, twiddle, second, last):
    outer = signal.shape[0]
    mid = table_left(first, jnp.concatenate([signal, response], axis=1))
    tw_real, tw_imag = twiddle[0], twiddle[1]
    turned = []
    for place in range(2):
        cols = slice(place * INNER, (place + 1) * INNER)
        real, imag = mid[:outer, cols], mid[outer:, cols]
        turned.append(jnp.concatenate(
            [real * tw_real - imag * tw_imag, real * tw_imag + imag * tw_real], axis=1
        ))
    spectra = table_right(jnp.concatenate(turned, axis=0), second)
    s_real, s_imag = spectra[:outer, :INNER], spectra[:outer, INNER:]
    r_real, r_imag = spectra[outer:, :INNER], spectra[outer:, INNER:]
    prod = jnp.concatenate(
        [s_real * r_real - s_imag * r_imag, -(s_real * r_imag + s_imag * r_real)], axis=1
    )
    back = table_right(prod, second)
    real, imag = back[:, :INNER], back[:, INNER:]
    turned = jnp.concatenate(
        [real * tw_real - imag * tw_imag, imag * tw_real + real * tw_imag], axis=0
    )
    return table_left(last, turned)


MESH_ID = pl.DeviceIdType.MESH
DEPTH = 1
LAG = 1


def partners(groups):
    return list(range(groups // 2, groups)) + list(range(1, groups // 2))


def flip(index, mask):
    bit = 1
    while bit <= mask:
        if mask & bit:
            index = index + bit - 2 * bit * ((index // bit) % 2)
        bit *= 2
    return index


def layer_kernel(
    groups, own_rows, chans, signal, response, gating, skip, weight,
    first, twiddle, second, last, out,
    send, held, made, conv, mixed, wall, wturn,
    fwd_send, fwd_recv, back_send, back_recv, own_sem, row_send, row_recv, w_send, w_recv, sib_sem, sib_recv, rel_send, rel_recv,
):
    chan_rows = groups * own_rows
    tiles_in = signal.shape[1]
    samples = tiles_in * 128
    pieces = samples // INNER
    chips = chans // 2
    me = lax.axis_index("seq")
    mine = lax.axis_index("chan")
    chip, core = mine // 2, mine % 2
    sibling = chip * 2 + 1 - core
    out_rows = out.shape[0]
    order = partners(groups)

    barrier = pltpu.get_barrier_semaphore()
    for mask in order:
        pl.semaphore_signal(barrier, inc=1, device_id={"seq": flip(me, mask)}, device_id_type=MESH_ID)
    for off in range(1, chans):
        pl.semaphore_signal(barrier, inc=1, device_id={"chan": lax.rem(mine + off, chans)}, device_id_type=MESH_ID)
    pl.semaphore_wait(barrier, groups + chans - 2)

    def forward(j, mask):
        return pltpu.make_async_remote_copy(
            send.at[j, flip(me, mask)], held.at[j, me], fwd_send.at[j, mask - 1], fwd_recv.at[j, mask - 1],
            device_id={"seq": flip(me, mask)}, device_id_type=MESH_ID)

    def arrived(j, who):
        size = 2 * pieces
        return conv.at[pl.ds(pl.multiple_of((j * groups + who) * size, size), size), :]

    def leaving(j, who):
        size = 2 * pieces
        return made.at[pl.ds(pl.multiple_of((j * groups + who) * size, size), size), :]

    def backward(j, mask):
        return pltpu.make_async_remote_copy(
            leaving(j, flip(me, mask)), arrived(j, me), back_send.at[j, mask - 1], back_recv.at[j, mask - 1],
            device_id={"seq": flip(me, mask)}, device_id_type=MESH_ID)

    def own_in(j):
        return pltpu.make_async_copy(send.at[j, me], held.at[j, me], own_sem.at[0, j])

    def own_back(j):
        return pltpu.make_async_copy(leaving(j, me), arrived(j, me), own_sem.at[1, j])

    bands = groups // 8

    def chunk(who, j):
        return mixed.at[pl.ds((who * own_rows + j) * bands, bands)]

    def to_sibling(j):
        return pltpu.make_async_remote_copy(
            chunk(mine, j), chunk(mine, j), sib_sem.at[j], sib_recv.at[j],
            device_id={"chan": sibling}, device_id_type=MESH_ID)

    def to_chip(j, off):
        return pltpu.make_async_remote_copy(
            chunk(mine, j), chunk(mine, j), row_send.at[j, off - 1], row_recv.at[j, off - 1],
            device_id={"chan": lax.rem(chip + off, chips) * 2 + core}, device_id_type=MESH_ID)

    def relay(j, off):
        who = lax.rem(chip + chips - off, chips) * 2 + core
        return pltpu.make_async_remote_copy(
            chunk(who, j), chunk(who, j), rel_send.at[j, off - 1], rel_recv.at[j, off - 1],
            device_id={"chan": sibling}, device_id_type=MESH_ID)

    own_weights = wall.at[pl.ds(pl.multiple_of(mine * chan_rows, 8), chan_rows), :]

    def weights(off):
        return pltpu.make_async_remote_copy(
            weight, own_weights, w_send.at[off - 1], w_recv.at[off - 1],
            device_id={"chan": lax.rem(mine + off, chans)}, device_id_type=MESH_ID)

    def launch(j):
        for g in range(groups):
            row = j * groups + g
            band, lane_row = row // 8, g % 8
            for place, ref in enumerate((signal, response)):
                for half in range(2):
                    send[j, g, place, :, half * 128:(half + 1) * 128] = ref[
                        band, pl.ds(half, pieces, stride=2), lane_row, :
                    ]
        for mask in order:
            forward(j, mask).start()
        own_in(j).start()

    def convolve(j):
        own_in(j).wait()
        for mask in order:
            forward(j, mask).wait_recv()
        rows = held[j]
        result = conv_row(
            rows[:, 0].reshape(groups * pieces, INNER), rows[:, 1].reshape(groups * pieces, INNER),
            first, twiddle, second, last,
        )
        for g in range(groups):
            for half in range(2):
                start = pl.multiple_of(((j * groups + g) * 2 + half) * pieces, pieces)
                made[pl.ds(start, pieces), :] = result[g * pieces:(g + 1) * pieces, half * 128:(half + 1) * 128]
        for mask in order:
            backward(j, mask).start()
        own_back(j).start()

    def gate(j):
        own_back(j).wait()
        for mask in order:
            backward(j, mask).wait_recv()
        for band in range(bands):
            here = j * bands + band
            gain = skip[pl.ds(pl.multiple_of(here * 8, 8), 8), :]
            for tile in range(tiles_in):
                start = (j * groups + band * 8) * 2 * pieces + (tile % 2) * pieces + tile // 2
                mixed[mine * own_rows * bands + here, tile] = gating[here, tile] * (
                    conv[pl.ds(start, 8, stride=2 * pieces), :] + gain * signal[here, tile]
                )
        to_sibling(j).start()
        for off in range(1, chips):
            to_chip(j, off).start()

    def pass_on(j):
        for off in range(1, chips):
            to_chip(j, off).wait_recv()
            relay(j, off).start()

    for j in range(min(DEPTH, own_rows)):
        launch(j)
    for off in range(1, chans):
        weights(off).start()
    wall[pl.ds(pl.multiple_of(mine * chan_rows, 8), chan_rows), :] = weight[...]

    @pl.loop(0, own_rows + LAG + 1)
    def _(t):
        @pl.when(t < own_rows)
        def _():
            for mask in order:
                forward(t, mask).wait_send()

            @pl.when(t + DEPTH < own_rows)
            def _():
                launch(t + DEPTH)

            convolve(t)

        @pl.when((t >= LAG) & (t < own_rows + LAG))
        def _():
            gate(t - LAG)

        @pl.when(t >= LAG + 1)
        def _():
            pass_on(t - LAG - 1)

    for off in range(1, chans):
        weights(off).wait()
    wturn[...] = jnp.transpose(wall[...])
    w_high, w_low = split(wturn[pl.ds(pl.multiple_of(mine * out_rows, 8), out_rows), :])
    w_both = jnp.concatenate([w_high, w_low], axis=0)

    @pl.loop(0, own_rows)
    def _(j):
        for mask in order:
            backward(j, mask).wait_send()
        to_sibling(j).wait()
        for off in range(1, chips):
            to_chip(j, off).wait_send()
            relay(j, off).wait()

    depth = chans * chan_rows

    @pl.loop(0, pieces)
    def _(i):
        data = jnp.concatenate([mixed[:, 2 * i + half].reshape(depth, 128) for half in range(2)], axis=1)
        high, low = split(data)
        both = matmul(w_both, high)
        out[:, pl.ds(pl.multiple_of(i * INNER, INNER), INNER)] = (
            both[:out_rows] + both[out_rows:] + matmul(w_high, low)
        )


def tiles(value):
    rows, columns = value.shape
    return value.reshape(rows // 8, 8, columns // 128, 128).transpose(0, 2, 1, 3)


def per_device(signal, gating, response, skip_gain, mixing_weight):
    chan_rows, samples = signal.shape
    groups = lax.axis_size("seq")
    chans = lax.axis_size("chan")
    own_rows = chan_rows // groups
    pieces = samples // INNER
    chips = chans // 2
    depth = mixing_weight.shape[0]
    out_rows = depth // chans
    consts = [jnp.asarray(t) for t in tables(groups * samples)]
    skip = jnp.broadcast_to(skip_gain[:, None], (chan_rows, 128))
    whole = pl.BlockSpec(memory_space=pltpu.VMEM)
    f32 = jnp.float32
    sems = pltpu.SemaphoreType.DMA
    return pl.pallas_call(
        partial(layer_kernel, groups, own_rows, chans),
        in_specs=[whole] * 9,
        out_specs=whole,
        out_shape=jax.ShapeDtypeStruct((out_rows, samples), f32),
        scratch_shapes=[
            pltpu.VMEM((own_rows, groups, 2, pieces, INNER), f32),
            pltpu.VMEM((own_rows, groups, 2, pieces, INNER), f32),
            pltpu.VMEM((chan_rows * 2 * pieces, 128), f32),
            pltpu.VMEM((chan_rows * 2 * pieces, 128), f32),
            pltpu.VMEM((chans * chan_rows // 8, samples // 128, 8, 128), f32),
            pltpu.VMEM((chans * chan_rows, depth), f32),
            pltpu.VMEM((depth, chans * chan_rows), f32),
            sems((own_rows, groups - 1)), sems((own_rows, groups - 1)),
            sems((own_rows, groups - 1)), sems((own_rows, groups - 1)),
            sems((2, own_rows)),
            sems((own_rows, chips - 1)), sems((own_rows, chips - 1)),
            sems((chans - 1,)), sems((chans - 1,)),
            sems((own_rows,)), sems((own_rows,)),
            sems((own_rows, chips - 1)), sems((own_rows, chips - 1)),
        ],
        compiler_params=pltpu.CompilerParams(
            collective_id=0, has_side_effects=True, vmem_limit_bytes=62 * 2**20
        ),
        name="layer",
    )(tiles(signal), tiles(response), tiles(gating), skip, mixing_weight.T, *consts)


def solution(mesh):
    in_specs = (P("chan", "seq"), P("chan", "seq"), P("chan", "seq"), P("chan"), P(None, "chan"))
    out_specs = P("chan", "seq")
    return jax.shard_map(
        per_device, mesh=mesh, in_specs=in_specs, out_specs=out_specs, check_vma=False
    )
```

time: 197 us -> 169 us (0.86)
  Pallas kernels: 188 us -> 164 us
  local copies, waits for them, and re-layouts: 7.31 us -> 4.4 us
    pallas_call x1, Pallas kernels: 188 us -> 164 us  [per_device(): pl.pallas_call(partial(layer_kernel, groups, own_rows, chans), in_specs=[...]
where the time goes in v3:
time: 169 us
  Pallas kernels  164 us (97%)
  local copies, waits for them, and re-layouts  4.4 us (3%)
    pallas_call x1, Pallas kernels, per_device(): pl.pallas_call(partial(layer_kernel, groups, own_rows, chans), in_specs=[...  164 us

profile of v3, /device:TPU:0, one launch (start us, length us, event | category | flops | bytes accessed | tf_op | source)
XLA Modules:
  0.0 168.6 jit_solution(6727679814921662725)
XLA Ops:
  0.0 1.3 broadcast_in_dim.2.skip
  1.3 164.2 %layer.1 = f32[64,8192]{1,0:T(8,128)} custom-call(f32[8,64,8,128]{3,2,1,0:T(8,128)} %bitcast.10, f32[8,64,8,128]{3,2,1,0:T(8,128)} %bitcast.11, f32[8,64,8,128]{3,2,1,0:T(8,128)} %bitcast.12, f32[64,128]{1,0:T(8,128)} %broadcast_in_dim.2.skip, f32[64,256]{1,0:T(8,128)} %bitcast.13, bf16[512,512]{1,0:T(8,128)(2,1)} %constant.8.clone.first, ...), custom_call_target="tpu_custom_call" | custom-call | tf_op jit(solution)/shard_map/layer/pallas_call | solution.py:302
  165.5 3.1 %copy.11 = f32[64,8192]{1,0:T(8,128)} copy(f32[64,8192]{1,0:T(8,128)} %layer.1) | data formatting | bytes 4194304
